TPU v7x, 32 devices: a whole 2x2x4 slice. The times are simulated.
32 devices in a mesh: runs: 2 (over y), gx: 4 (over z), gy: 2 (over core), gz: 2 (over x).
Axes of the slice: x: 2, y: 2, z: 4, core: 2. Of those that a mesh axis runs over, the one named last changes fastest.
Arguments:
- labels: int32 [24, 128, 1024], P(('runs', 'gz'), 'gx', 'gy'), parts along dimension 0, may hold values from 0 to 3
- background: bfloat16 [24, 128, 1024], P(('runs', 'gz'), 'gx', 'gy'), parts along dimension 0, may hold values from -3 to 3
- contrasts: float32 [8], P('runs'), parts along dimension 0, may hold values from -1 to 1
- kernels: bfloat16 [24, 15, 15], P(('runs', 'gz')), parts along dimension 0, may hold values from -0.125 to 0.125
- observed: float32 [6, 128, 1024], P('runs', 'gx', 'gy'), parts along dimension 0, may hold values from -6 to 6
Outputs:
- residual: float32 [6, 128, 1024], P('runs', ('gx', 'gz'), 'gy'), parts along dimension 0
- gradient: float32 [24, 128, 1024], P(('runs', 'gz'), 'gx', 'gy'), parts along dimension 0
There are 2 independent parts, one for each index of `runs`. A program takes and returns all parts, laid end to end along the dimension named above; each array names one. Nothing has to cross between parts.
All inputs are finite; a program needn't handle non-finite values.
Results may differ from a plain program's by a relative error of at most 0.0058.
Values may be sent and summed in bfloat16 or wider, within the bound.
No kernel may reach another device: no remote copies, remote signals or barrier semaphores. Data moves between devices by JAX's collectives and lax.ppermute only.
A program may use at most 64 MiB of HBM per device.

v0:
```python
import jax
import jax.numpy as jnp
from jax import lax
from jax.sharding import PartitionSpec as P

ITERS = 2
descent = 0.01


def padded_2(value, sides, width):
    for axis, dim in sides:
        peers, length = (lax.axis_size(axis), value.shape[dim])
        up = [(i, (i + 1) % peers) for i in range(peers)]
        down = [(j, i) for i, j in up]
        last = lax.slice_in_dim(value, length - width, length, axis=dim)
        initial = lax.slice_in_dim(value, 0, width, axis=dim)
        before = lax.ppermute(last, axis, up)
        after = lax.ppermute(initial, axis, down)
        value = jnp.concatenate([before, value, after], axis=dim)
    return value


def band_selector(span, block_width):
    shape = (span, 2 * block_width, block_width)
    offset = lax.broadcasted_iota(jnp.int32, shape, 1) - lax.broadcasted_iota(jnp.int32, shape, 2)
    return jnp.where(offset == lax.broadcasted_iota(jnp.int32, shape, 0), 1.0, 0.0).astype(
        jnp.bfloat16
    )


def band_matrices(kernel, selector):
    summed = jnp.einsum("sc,cpq->spq", kernel, selector, preferred_element_type=jnp.float32)
    return summed.astype(jnp.bfloat16)


def banded_sum(padded, band_rows, row_count, blocks, block_width):
    pieces = []
    for row_shift in range(band_rows.shape[0]):
        window = padded[row_shift : row_shift + row_count]
        pieces.append(window[:, : blocks * block_width].reshape(row_count, blocks, block_width))
        pieces.append(
            window[:, block_width : (blocks + 1) * block_width].reshape(
                row_count, blocks, block_width
            )
        )
    stacked = jnp.concatenate(pieces, axis=2)
    weights = band_rows.reshape(band_rows.shape[0] * 2 * block_width, block_width)
    summed = jnp.einsum("rbk,kq->rbq", stacked, weights, preferred_element_type=jnp.float32)
    return summed.reshape(row_count, blocks * block_width)


def surface_halo(rounded, kernels, selector, block_width, blocks, radius):
    depth_count, cells_x, cells_y = rounded.shape
    padded = padded_2(rounded, (("gx", 1), ("gy", 2)), radius)
    padded = jnp.pad(padded, ((0, 0), (0, 0), (0, block_width - 2 * radius)))

    def add_layer(depth_index, summed):
        band_rows = band_matrices(
            lax.dynamic_index_in_dim(kernels, depth_index, 0, keepdims=False), selector
        )
        layer_cells = lax.dynamic_index_in_dim(padded, depth_index, 0, keepdims=False)
        return summed + banded_sum(layer_cells, band_rows, cells_x, blocks, block_width)

    return lax.fori_loop(0, depth_count, add_layer, jnp.zeros((cells_x, cells_y), jnp.float32))


def tensor_parts(edged_values):
    centre = edged_values[..., 1:-1, 1:-1]
    along_x = edged_values[..., 2:, 1:-1] + edged_values[..., :-2, 1:-1] - 2.0 * centre
    along_y = edged_values[..., 1:-1, 2:] + edged_values[..., 1:-1, :-2] - 2.0 * centre
    mixed = 0.25 * (
        edged_values[..., 2:, 2:]
        - edged_values[..., 2:, :-2]
        - edged_values[..., :-2, 2:]
        + edged_values[..., :-2, :-2]
    )
    return (along_x, along_y, mixed)


def adjoint_sum(edged_misfit):
    return (
        tensor_parts(edged_misfit[0])[0]
        + tensor_parts(edged_misfit[1])[1]
        + tensor_parts(edged_misfit[2])[2]
    )


def layer_gradients(adjoint_field, flipped, selector, block_width, blocks, radius):
    depth_count = flipped.shape[0]
    cells_x, cells_y = adjoint_field.shape
    padded = padded_2(adjoint_field, (("gx", 0), ("gy", 1)), radius)
    padded = jnp.pad(padded, ((0, 0), (0, block_width - 2 * radius)))

    def one_layer(depth_index, stacked):
        band_rows = band_matrices(
            lax.dynamic_index_in_dim(flipped, depth_index, 0, keepdims=False), selector
        )
        layer_grad = banded_sum(padded, band_rows, cells_x, blocks, block_width)
        return lax.dynamic_update_index_in_dim(stacked, layer_grad, depth_index, 0)

    return lax.fori_loop(
        0, depth_count, one_layer, jnp.zeros((depth_count, cells_x, cells_y), jnp.float32)
    )


def body(labels, background, contrasts, kernels, observed):
    cells_x = labels.shape[1]
    cells_y = labels.shape[2]
    block_width = min(cells_y, 128)
    blocks = cells_y // block_width
    radius = (kernels.shape[1] - 1) // 2
    share_rows = cells_x // lax.axis_size("gz")
    selector = band_selector(kernels.shape[2], block_width)
    flipped = kernels[:, ::-1, ::-1]
    density = background.astype(jnp.float32)
    for class_id in range(contrasts.shape[0]):
        density = density + jnp.where(labels == class_id, contrasts[class_id], 0.0)
    residual = observed[:, :share_rows]
    gradient = density
    for iteration in range(ITERS):
        rounded = density.astype(jnp.bfloat16)
        partial_value = surface_halo(rounded, kernels, selector, block_width, blocks, radius)
        surface = lax.psum(partial_value, "gz")
        edged_surface = padded_2(surface, (("gx", 0), ("gy", 1)), 1)
        misfit = jnp.stack(tensor_parts(edged_surface)) - observed
        edged_misfit = padded_2(misfit, (("gx", 1), ("gy", 2)), 1)
        adjoint_field = adjoint_sum(edged_misfit).astype(jnp.bfloat16)
        residual = lax.dynamic_slice_in_dim(
            misfit, lax.axis_index("gz") * share_rows, share_rows, 1
        )
        gradient = layer_gradients(adjoint_field, flipped, selector, block_width, blocks, radius)
        density = density - descent * gradient
    return (residual, gradient)


def solution(mesh):
    placed = (
        P(("runs", "gz"), "gx", "gy"),
        P(("runs", "gz"), "gx", "gy"),
        P("runs"),
        P(("runs", "gz"), None, None),
        P("runs", "gx", "gy"),
    )
    return jax.shard_map(
        body,
        mesh=mesh,
        in_specs=placed,
        out_specs=(P("runs", ("gx", "gz"), "gy"), P(("runs", "gz"), "gx", "gy")),
        check_vma=False,
    )
```

profile of v0, /device:TPU:0, one launch (start us, length us, event | category | flops | bytes accessed | tf_op | source)
XLA Modules:
  0.0 187.0 jit_solution(16644792273264350666)
XLA Ops:
  8.6 3.6 %fusion.98 = bf16[6,32,512]{2,1,0:T(8,128)(2,1)S(1)} fusion(f32[]{:T(128)} %bitcast.3, s32[6,32,512]{2,1,0:T(8,128)} %param.13, f32[]{:T(128)} %bitcast.2, f32[]{:T(128)} %bitcast.1, f32[]{:T(128)} %bitcast, bf16[6,32,512]{2,1,0:T(8,128)(2,1)} %param.14), kind=kLoop, calls=%fused_computation.448 | loop fusion | flops 1376256 | bytes 786448 | tf_op jit(solution)/shard_map/convert_element_type | solution.py:121
  12.2 3.1 %collective-permute-start = (bf16[6,7,512]{2,1,0:T(8,128)(2,1)S(1)}, bf16[6,7,512]{2,1,0:T(8,128)(2,1)S(1)}, u32[]{:S(2)}, u32[]{:S(2)}) collective-permute-start(bf16[6,7,512]{2,1,0:T(8,128)(2,1)S(1)} %get-tuple-element.678), channel_id=1, source_target_pairs={{0,4},{4,8},{8,12},{12,0},{1,5},{5,9},{9,13},{13,1},{2,6},{6,10},{... | collective-permute-start | bytes 129032 | tf_op jit(solution)/shard_map/ppermute | solution.py:17
  15.3 2.1 %collective-permute-start.1 = (bf16[6,7,512]{2,1,0:T(8,128)(2,1)S(1)}, bf16[6,7,512]{2,1,0:T(8,128)(2,1)S(1)}, u32[]{:S(2)}, u32[]{:S(2)}) collective-permute-start(bf16[6,7,512]{2,1,0:T(8,128)(2,1)S(1)} %get-tuple-element.679), channel_id=1, source_target_pairs={{4,0},{8,4},{12,8},{0,12},{5,1},{9,5},{13,9},{1,13},{6,2},{10,6},{... | collective-permute-start | bytes 129032 | tf_op jit(solution)/shard_map/ppermute | solution.py:18
  17.4 2.1 %collective-permute-done = bf16[6,7,512]{2,1,0:T(8,128)(2,1)S(1)} collective-permute-done((bf16[6,7,512]{2,1,0:T(8,128)(2,1)S(1)}, bf16[6,7,512]{2,1,0:T(8,128)(2,1)S(1)}, u32[]{:S(2)}, u32[]{:S(2)}) %collective-permute-start) | collective-permute-done | bytes 43040 | tf_op jit(solution)/shard_map/ppermute | solution.py:17
  21.9 13.9 %while.62 = (s32[]{:T(128)}, f32[32,512]{1,0:T(8,128)S(1)}, bf16[6,46,640]{2,1,0:T(8,128)(2,1)S(1)}, bf16[6,15,15]{2,1,0:T(8,128)(2,1)S(1)}, s32[]{:T(128)}, /*i...) while((s32[]{:T(128)}, f32[32,512]{1,0:T(8,128)S(1)}, ...), condition=%wide.region_1.2_spmd.clone, body=%wide.region_0.1_spmd.clone.sunk | while | flops 143065104 | bytes 10342823 | solution.py:64
  36.6 22.2 %all-reduce.7.cloned.1.call-done = f32[32,512]{1,0:T(8,128)} async-done(((f32[32,512]{1,0:T(8,128)}), f32[32,512]{1,0:T(8,128)}) %all-reduce.7.cloned.1.call-update) | async-done | bytes 65552 | tf_op jit(solution)/shard_map/psum | solution.py:123
  59.5 3.3 %collective-permute-start.4 = (f32[1,512]{1,0:T(1,128)S(1)}, f32[1,512]{1,0:T(1,128)S(1)}, u32[]{:S(2)}, u32[]{:S(2)}) collective-permute-start(f32[1,512]{1,0:T(1,128)S(1)} %get-tuple-element.693), channel_id=1, source_target_pairs={{4,0},{8,4},{12,8},{0,12},{5,1},{9,5},{13,9},{1,13},{6,2},{10,6},{... | collective-permute-start | bytes 6152 | tf_op jit(solution)/shard_map/ppermute | solution.py:18
  64.1 4.1 %collective-permute-done.5 = f32[1,512]{1,0:T(1,128)S(1)} collective-permute-done((f32[1,512]{1,0:T(1,128)S(1)}, f32[1,512]{1,0:T(1,128)S(1)}, u32[]{:S(2)}, u32[]{:S(2)}) %collective-permute-start.5) | collective-permute-done | bytes 2080 | tf_op jit(solution)/shard_map/ppermute | solution.py:17
  72.6 3.8 %collective-permute-start.9 = (f32[3,1,512]{2,1,0:T(1,128)S(1)}, f32[3,1,512]{2,1,0:T(1,128)S(1)}, u32[]{:S(2)}, u32[]{:S(2)}) collective-permute-start(f32[3,1,512]{2,1,0:T(1,128)S(1)} %get-tuple-element.677), channel_id=1, source_target_pairs={{4,0},{8,4},{12,8},{0,12},{5,1},{9,5},{13,9},{1,13},{6,2},{10,6},{... | collective-permute-start | bytes 18440 | tf_op jit(solution)/shard_map/ppermute | solution.py:18
  76.4 1.6 collective-permute-done.8
  80.1 3.9 %collective-permute-start.13 = (bf16[7,512]{1,0:T(8,128)(2,1)S(1)}, bf16[7,512]{1,0:T(8,128)(2,1)S(1)}, u32[]{:S(2)}, u32[]{:S(2)}) collective-permute-start(bf16[7,512]{1,0:T(8,128)(2,1)S(1)} %get-tuple-element.761), channel_id=1, source_target_pairs={{4,0},{8,4},{12,8},{0,12},{5,1},{9,5},{13,9},{1,13},{6,2},{10,6},{... | collective-permute-start | bytes 21512 | tf_op jit(solution)/shard_map/ppermute | solution.py:18
  84.0 1.6 collective-permute-done.12
  88.1 7.6 %while.60 = (s32[]{:T(128)}, f32[6,32,512]{2,1,0:T(8,128)S(1)}, bf16[6,15,15]{2,1,0:T(8,128)(2,1)S(1)}, bf16[32,4,3840]{2,0,1:T(8,128)(2,1)S(1)}, s32[]{:T(128)}) while((s32[]{:T(128)}, f32[6,32,512]{2,1,0:T(8,128)S(1)}, bf16[6,15,15]{2,1,0:T(8,128)(2,1)S(1)}, bf16[32,4,3840]{2,0,1:T(8,128)(2,1)S(1)}, s32[]{:T(128)}) %tuple.339), condition=%wide.region_4.5_spmd.clone, body=%wide.region_3.4_spmd.clone.sunk | while | flops 143032320 | bytes 5378117 | solution.py:101
  95.7 2.6 %subtract_convert_fusion = bf16[6,32,512]{2,1,0:T(8,128)(2,1)S(1)} fusion(f32[6,32,512]{2,1,0:T(8,128)S(1)} %get-tuple-element.447, f32[]{:T(128)} %bitcast.3, s32[6,32,512]{2,1,0:T(8,128)S(1)} %copy-done.2, f32[]{:T(128)} %bitcast.2, f32[]{:T(128)} %bitcast.1, f32[]{:T(128)} %bitcast, bf16[6,32,512]{2,1,0:T(8,128)(2,1)S(1)} %copy-done.3), kind=kLoop, calls=%fused_computation.213 | loop fusion | flops 1572864 | bytes 1179664 | tf_op jit(solution)/shard_map/convert_element_type | solution.py:121
  99.5 2.8 %collective-permute-start.17 = (bf16[6,7,512]{2,1,0:T(8,128)(2,1)S(1)}, bf16[6,7,512]{2,1,0:T(8,128)(2,1)S(1)}, u32[]{:S(2)}, u32[]{:S(2)}) collective-permute-start(bf16[6,7,512]{2,1,0:T(8,128)(2,1)S(1)} %get-tuple-element.675), channel_id=1, source_target_pairs={{4,0},{8,4},{12,8},{0,12},{5,1},{9,5},{13,9},{1,13},{6,2},{10,6},{... | collective-permute-start | bytes 129032 | tf_op jit(solution)/shard_map/ppermute | solution.py:18
  102.3 2.3 %collective-permute-done.16 = bf16[6,7,512]{2,1,0:T(8,128)(2,1)S(1)} collective-permute-done((bf16[6,7,512]{2,1,0:T(8,128)(2,1)S(1)}, bf16[6,7,512]{2,1,0:T(8,128)(2,1)S(1)}, u32[]{:S(2)}, u32[]{:S(2)}) %collective-permute-start.16) | collective-permute-done | bytes 43040 | tf_op jit(solution)/shard_map/ppermute | solution.py:17
  106.5 14.0 %while.63 = (s32[]{:T(128)}, f32[32,512]{1,0:T(8,128)S(1)}, bf16[6,46,640]{2,1,0:T(8,128)(2,1)S(1)}, bf16[6,15,15]{2,1,0:T(8,128)(2,1)S(1)}, s32[]{:T(128)}, /*i...) while((s32[]{:T(128)}, f32[32,512]{1,0:T(8,128)S(1)}, ...), condition=%wide.region_6.7_spmd.clone, body=%wide.region_5.6_spmd.clone.sunk | while | flops 143065104 | bytes 10342823 | solution.py:64
  121.2 21.3 %all-reduce.9.cloned.1.call-done = f32[32,512]{1,0:T(8,128)} async-done(((f32[32,512]{1,0:T(8,128)}), f32[32,512]{1,0:T(8,128)}) %all-reduce.9.cloned.1.call-update) | async-done | bytes 65552 | tf_op jit(solution)/shard_map/psum | solution.py:123
  143.2 3.3 %collective-permute-start.20 = (f32[1,512]{1,0:T(1,128)S(1)}, f32[1,512]{1,0:T(1,128)S(1)}, u32[]{:S(2)}, u32[]{:S(2)}) collective-permute-start(f32[1,512]{1,0:T(1,128)S(1)} %get-tuple-element.690), channel_id=1, source_target_pairs={{4,0},{8,4},{12,8},{0,12},{5,1},{9,5},{13,9},{1,13},{6,2},{10,6},{... | collective-permute-start | bytes 6152 | tf_op jit(solution)/shard_map/ppermute | solution.py:18
  147.9 4.1 %collective-permute-done.21 = f32[1,512]{1,0:T(1,128)S(1)} collective-permute-done((f32[1,512]{1,0:T(1,128)S(1)}, f32[1,512]{1,0:T(1,128)S(1)}, u32[]{:S(2)}, u32[]{:S(2)}) %collective-permute-start.21) | collective-permute-done | bytes 2080 | tf_op jit(solution)/shard_map/ppermute | solution.py:17
  156.3 3.8 %collective-permute-start.25 = (f32[3,1,512]{2,1,0:T(1,128)S(1)}, f32[3,1,512]{2,1,0:T(1,128)S(1)}, u32[]{:S(2)}, u32[]{:S(2)}) collective-permute-start(f32[3,1,512]{2,1,0:T(1,128)S(1)} %get-tuple-element.673), channel_id=1, source_target_pairs={{4,0},{8,4},{12,8},{0,12},{5,1},{9,5},{13,9},{1,13},{6,2},{10,6},{... | collective-permute-start | bytes 18440 | tf_op jit(solution)/shard_map/ppermute | solution.py:18
  160.1 1.6 collective-permute-done.24
  163.8 3.9 %collective-permute-start.29 = (bf16[7,512]{1,0:T(8,128)(2,1)S(1)}, bf16[7,512]{1,0:T(8,128)(2,1)S(1)}, u32[]{:S(2)}, u32[]{:S(2)}) collective-permute-start(bf16[7,512]{1,0:T(8,128)(2,1)S(1)} %get-tuple-element.759), channel_id=1, source_target_pairs={{4,0},{8,4},{12,8},{0,12},{5,1},{9,5},{13,9},{1,13},{6,2},{10,6},{... | collective-permute-start | bytes 21512 | tf_op jit(solution)/shard_map/ppermute | solution.py:18
  171.8 7.6 %while.61 = (s32[]{:T(128)}, f32[6,32,512]{2,1,0:T(8,128)S(1)}, bf16[6,15,15]{2,1,0:T(8,128)(2,1)S(1)}, bf16[32,4,3840]{2,0,1:T(8,128)(2,1)S(1)}, s32[]{:T(128)}) while((s32[]{:T(128)}, f32[6,32,512]{2,1,0:T(8,128)S(1)}, bf16[6,15,15]{2,1,0:T(8,128)(2,1)S(1)}, bf16[32,4,3840]{2,0,1:T(8,128)(2,1)S(1)}, s32[]{:T(128)}) %tuple.354), condition=%wide.region_9.10_spmd.clone, body=%wide.region_8.9_spmd.clone.sunk | while | flops 143032320 | bytes 5378117 | solution.py:101
  (759 shorter events, 70.4 us)
Async XLA Ops:
  7.2 51.6 %all-reduce.7.cloned.1.call-start = ((), (), s32[]{:S(2)}) async-start(), calls=%async_computation | async-start | bytes 131072 | tf_op jit(solution)/shard_map/psum | solution.py:123
  12.2 7.3 %collective-permute-start = (bf16[6,7,512]{2,1,0:T(8,128)(2,1)S(1)}, bf16[6,7,512]{2,1,0:T(8,128)(2,1)S(1)}, u32[]{:S(2)}, u32[]{:S(2)}) collective-permute-start(bf16[6,7,512]{2,1,0:T(8,128)(2,1)S(1)} %get-tuple-element.678), channel_id=1, source_target_pairs={{0,4},{4,8},{8,12},{12,0},{1,5},{5,9},{9,13},{13,1},{2,6},{6,10},{... | collective-permute-start | bytes 129032 | tf_op jit(solution)/shard_map/ppermute | solution.py:17
  15.3 4.6 %collective-permute-start.1 = (bf16[6,7,512]{2,1,0:T(8,128)(2,1)S(1)}, bf16[6,7,512]{2,1,0:T(8,128)(2,1)S(1)}, u32[]{:S(2)}, u32[]{:S(2)}) collective-permute-start(bf16[6,7,512]{2,1,0:T(8,128)(2,1)S(1)} %get-tuple-element.679), channel_id=1, source_target_pairs={{4,0},{8,4},{12,8},{0,12},{5,1},{9,5},{13,9},{1,13},{6,2},{10,6},{... | collective-permute-start | bytes 129032 | tf_op jit(solution)/shard_map/ppermute | solution.py:18
  20.2 1.4 collective-permute-start.3
  36.5 106.0 %all-reduce.9.cloned.1.call-start = ((), (), s32[]{:S(2)}) async-start(), calls=%async_computation.1 | async-start | bytes 131072 | tf_op jit(solution)/shard_map/psum | solution.py:123
  59.5 4.6 %collective-permute-start.4 = (f32[1,512]{1,0:T(1,128)S(1)}, f32[1,512]{1,0:T(1,128)S(1)}, u32[]{:S(2)}, u32[]{:S(2)}) collective-permute-start(f32[1,512]{1,0:T(1,128)S(1)} %get-tuple-element.693), channel_id=1, source_target_pairs={{4,0},{8,4},{12,8},{0,12},{5,1},{9,5},{13,9},{1,13},{6,2},{10,6},{... | collective-permute-start | bytes 6152 | tf_op jit(solution)/shard_map/ppermute | solution.py:18
  62.8 5.4 %collective-permute-start.5 = (f32[1,512]{1,0:T(1,128)S(1)}, f32[1,512]{1,0:T(1,128)S(1)}, u32[]{:S(2)}, u32[]{:S(2)}) collective-permute-start(f32[1,512]{1,0:T(1,128)S(1)} %get-tuple-element.692), channel_id=1, source_target_pairs={{0,4},{4,8},{8,12},{12,0},{1,5},{5,9},{9,13},{13,1},{2,6},{6,10},{... | collective-permute-start | bytes 6152 | tf_op jit(solution)/shard_map/ppermute | solution.py:17
  69.1 1.3 collective-permute-start.7
  72.6 5.5 %collective-permute-start.8 = (f32[3,1,512]{2,1,0:T(1,128)S(1)}, f32[3,1,512]{2,1,0:T(1,128)S(1)}, u32[]{:S(2)}, u32[]{:S(2)}) collective-permute-start(f32[3,1,512]{2,1,0:T(1,128)S(1)} %get-tuple-element.676), channel_id=1, source_target_pairs={{0,4},{4,8},{8,12},{12,0},{1,5},{5,9},{9,13},{13,1},{2,6},{6,10},{... | collective-permute-start | bytes 18440 | tf_op jit(solution)/shard_map/ppermute | solution.py:17
  72.6 5.4 %collective-permute-start.9 = (f32[3,1,512]{2,1,0:T(1,128)S(1)}, f32[3,1,512]{2,1,0:T(1,128)S(1)}, u32[]{:S(2)}, u32[]{:S(2)}) collective-permute-start(f32[3,1,512]{2,1,0:T(1,128)S(1)} %get-tuple-element.677), channel_id=1, source_target_pairs={{4,0},{8,4},{12,8},{0,12},{5,1},{9,5},{13,9},{1,13},{6,2},{10,6},{... | collective-permute-start | bytes 18440 | tf_op jit(solution)/shard_map/ppermute | solution.py:18
  78.2 1.4 collective-permute-start.11
  80.1 5.5 %collective-permute-start.12 = (bf16[7,512]{1,0:T(8,128)(2,1)S(1)}, bf16[7,512]{1,0:T(8,128)(2,1)S(1)}, u32[]{:S(2)}, u32[]{:S(2)}) collective-permute-start(bf16[7,512]{1,0:T(8,128)(2,1)S(1)} %get-tuple-element.760), channel_id=1, source_target_pairs={{0,4},{4,8},{8,12},{12,0},{1,5},{5,9},{9,13},{13,1},{2,6},{6,10},{... | collective-permute-start | bytes 21512 | tf_op jit(solution)/shard_map/ppermute | solution.py:17
  80.1 5.5 %collective-permute-start.13 = (bf16[7,512]{1,0:T(8,128)(2,1)S(1)}, bf16[7,512]{1,0:T(8,128)(2,1)S(1)}, u32[]{:S(2)}, u32[]{:S(2)}) collective-permute-start(bf16[7,512]{1,0:T(8,128)(2,1)S(1)} %get-tuple-element.761), channel_id=1, source_target_pairs={{4,0},{8,4},{12,8},{0,12},{5,1},{9,5},{13,9},{1,13},{6,2},{10,6},{... | collective-permute-start | bytes 21512 | tf_op jit(solution)/shard_map/ppermute | solution.py:18
  98.3 6.3 %collective-permute-start.16 = (bf16[6,7,512]{2,1,0:T(8,128)(2,1)S(1)}, bf16[6,7,512]{2,1,0:T(8,128)(2,1)S(1)}, u32[]{:S(2)}, u32[]{:S(2)}) collective-permute-start(bf16[6,7,512]{2,1,0:T(8,128)(2,1)S(1)} %get-tuple-element.674), channel_id=1, source_target_pairs={{0,4},{4,8},{8,12},{12,0},{1,5},{5,9},{9,13},{13,1},{2,6},{6,10},{... | collective-permute-start | bytes 129032 | tf_op jit(solution)/shard_map/ppermute | solution.py:17
  99.5 5.1 %collective-permute-start.17 = (bf16[6,7,512]{2,1,0:T(8,128)(2,1)S(1)}, bf16[6,7,512]{2,1,0:T(8,128)(2,1)S(1)}, u32[]{:S(2)}, u32[]{:S(2)}) collective-permute-start(bf16[6,7,512]{2,1,0:T(8,128)(2,1)S(1)} %get-tuple-element.675), channel_id=1, source_target_pairs={{4,0},{8,4},{12,8},{0,12},{5,1},{9,5},{13,9},{1,13},{6,2},{10,6},{... | collective-permute-start | bytes 129032 | tf_op jit(solution)/shard_map/ppermute | solution.py:18
  104.8 1.4 collective-permute-start.19
  143.2 4.6 %collective-permute-start.20 = (f32[1,512]{1,0:T(1,128)S(1)}, f32[1,512]{1,0:T(1,128)S(1)}, u32[]{:S(2)}, u32[]{:S(2)}) collective-permute-start(f32[1,512]{1,0:T(1,128)S(1)} %get-tuple-element.690), channel_id=1, source_target_pairs={{4,0},{8,4},{12,8},{0,12},{5,1},{9,5},{13,9},{1,13},{6,2},{10,6},{... | collective-permute-start | bytes 6152 | tf_op jit(solution)/shard_map/ppermute | solution.py:18
  146.6 5.4 %collective-permute-start.21 = (f32[1,512]{1,0:T(1,128)S(1)}, f32[1,512]{1,0:T(1,128)S(1)}, u32[]{:S(2)}, u32[]{:S(2)}) collective-permute-start(f32[1,512]{1,0:T(1,128)S(1)} %get-tuple-element.689), channel_id=1, source_target_pairs={{0,4},{4,8},{8,12},{12,0},{1,5},{5,9},{9,13},{13,1},{2,6},{6,10},{... | collective-permute-start | bytes 6152 | tf_op jit(solution)/shard_map/ppermute | solution.py:17
  152.8 1.3 collective-permute-start.23
  156.3 5.5 %collective-permute-start.24 = (f32[3,1,512]{2,1,0:T(1,128)S(1)}, f32[3,1,512]{2,1,0:T(1,128)S(1)}, u32[]{:S(2)}, u32[]{:S(2)}) collective-permute-start(f32[3,1,512]{2,1,0:T(1,128)S(1)} %get-tuple-element.672), channel_id=1, source_target_pairs={{0,4},{4,8},{8,12},{12,0},{1,5},{5,9},{9,13},{13,1},{2,6},{6,10},{... | collective-permute-start | bytes 18440 | tf_op jit(solution)/shard_map/ppermute | solution.py:17
  156.3 5.4 %collective-permute-start.25 = (f32[3,1,512]{2,1,0:T(1,128)S(1)}, f32[3,1,512]{2,1,0:T(1,128)S(1)}, u32[]{:S(2)}, u32[]{:S(2)}) collective-permute-start(f32[3,1,512]{2,1,0:T(1,128)S(1)} %get-tuple-element.673), channel_id=1, source_target_pairs={{4,0},{8,4},{12,8},{0,12},{5,1},{9,5},{13,9},{1,13},{6,2},{10,6},{... | collective-permute-start | bytes 18440 | tf_op jit(solution)/shard_map/ppermute | solution.py:18
  161.9 1.4 collective-permute-start.27
  163.8 5.5 %collective-permute-start.28 = (bf16[7,512]{1,0:T(8,128)(2,1)S(1)}, bf16[7,512]{1,0:T(8,128)(2,1)S(1)}, u32[]{:S(2)}, u32[]{:S(2)}) collective-permute-start(bf16[7,512]{1,0:T(8,128)(2,1)S(1)} %get-tuple-element.758), channel_id=1, source_target_pairs={{0,4},{4,8},{8,12},{12,0},{1,5},{5,9},{9,13},{13,1},{2,6},{6,10},{... | collective-permute-start | bytes 21512 | tf_op jit(solution)/shard_map/ppermute | solution.py:17
  163.8 5.5 %collective-permute-start.29 = (bf16[7,512]{1,0:T(8,128)(2,1)S(1)}, bf16[7,512]{1,0:T(8,128)(2,1)S(1)}, u32[]{:S(2)}, u32[]{:S(2)}) collective-permute-start(bf16[7,512]{1,0:T(8,128)(2,1)S(1)} %get-tuple-element.759), channel_id=1, source_target_pairs={{4,0},{8,4},{12,8},{0,12},{5,1},{9,5},{13,9},{1,13},{6,2},{10,6},{... | collective-permute-start | bytes 21512 | tf_op jit(solution)/shard_map/ppermute | solution.py:18
  (17 other events, 79.8 us)
Sparse Core Ops, SparseCore 0:
  36.6 22.0 all-reduce.6
  121.3 21.1 all-reduce.8
where the time goes:
time: 188 us; the launch traced here: 187 us
  waiting for transfers between devices  71.8 us (38%)
  starting transfers between devices  35.8 us (19%)
  local copies, waits for them, and re-layouts  24.8 us (13%)
  matrix products  20.5 us (11%)
  between operations  14.9 us (8%)
  other arithmetic  14.6 us (8%)
  loops' own time  4.55 us (2%)
    psum x2, waiting for transfers between devices, body(): surface = lax.psum(partial_value, 'gz')  43.5 us
    ppermute x16, starting transfers between devices, padded_2(): after = lax.ppermute(initial, axis, down)  29.9 us
    ppermute x16, waiting for transfers between devices, padded_2(): before = lax.ppermute(last, axis, up)  22.8 us
    dot_general x24, matrix products, band_matrices(): jnp.einsum('sc,cpq->spq', kernel, selector, preferred_element_type=jnp.fl...  10.6 us
    dot_general x24, matrix products, banded_sum(): jnp.einsum('rbk,kq->rbq', stacked, weights, preferred_element_type=jnp.fl...  9.84 us
    while x444, local copies, waits for them, and re-layouts  6.95 us
    convert_element_type x24, local copies, waits for them, and re-layouts, band_matrices(): return summed.astype(jnp.bfloat16)  6.3 us
    convert_element_type x2, other arithmetic, body(): rounded = density.astype(jnp.bfloat16)  6.14 us
  transfers between devices with their start and end apart: 34, of which 28 were waited for; matrix products, arithmetic and copies ran while one was open for 0% of the time, Pallas kernels for 0%

commit v1 on v0

--- a/solution.py
+++ b/solution.py
@@ -120,7 +120,7 @@
     for iteration in range(ITERS):
         rounded = density.astype(jnp.bfloat16)
         partial_value = surface_halo(rounded, kernels, selector, block_width, blocks, radius)
-        surface = lax.psum(partial_value, "gz")
+        surface = jnp.sum(lax.all_gather(partial_value, "gz"), axis=0)
         edged_surface = padded_2(surface, (("gx", 0), ("gy", 1)), 1)
         misfit = jnp.stack(tensor_parts(edged_surface)) - observed
         edged_misfit = padded_2(misfit, (("gx", 1), ("gy", 2)), 1)

time: 188 us -> 133 us (0.71)
  waiting for transfers between devices: 71.8 us -> 28.2 us
  between operations: 14.9 us -> 1.52 us
  blocking collectives: 0 us -> 10.2 us
  other arithmetic: 14.6 us -> 9.72 us
  local copies, waits for them, and re-layouts: 24.8 us -> 22.1 us
    psum x2 -> x0, waiting for transfers between devices: 43.5 us -> none  [body(): surface = lax.psum(partial_value, 'gz')]
    all_gather x0 -> x2, blocking collectives: none -> 10.2 us  [body(): surface = jnp.sum(lax.all_gather(partial_value, 'gz'), axis=0)]
    another operation x2, other arithmetic: 2.15 us -> 0.24 us  [body(): misfit = jnp.stack(tensor_parts(edged_surface)) - observed]
  transfers between devices with their start and end apart: 34 -> 32, of which waited for: 28 -> 26; matrix products, arithmetic and copies ran while one was open for 0% -> 1% of each run, Pallas kernels for 0% -> 0%
where the time goes in v1:
time: 133 us
  starting transfers between devices  36.1 us (27%)
  waiting for transfers between devices  28.2 us (21%)
  local copies, waits for them, and re-layouts  22.1 us (17%)
  matrix products  20.5 us (15%)
  blocking collectives  10.2 us (8%)
  other arithmetic  9.72 us (7%)
  loops' own time  4.56 us (3%)
  between operations  1.52 us (1%)
    ppermute x16, starting transfers between devices, padded_2(): after = lax.ppermute(initial, axis, down)  30.3 us
    ppermute x16, waiting for transfers between devices, padded_2(): before = lax.ppermute(last, axis, up)  22.8 us
    dot_general x24, matrix products, band_matrices(): jnp.einsum('sc,cpq->spq', kernel, selector, preferred_element_type=jnp.fl...  10.6 us
    all_gather x2, blocking collectives, body(): surface = jnp.sum(lax.all_gather(partial_value, 'gz'), axis=0)  10.2 us
    dot_general x24, matrix products, banded_sum(): jnp.einsum('rbk,kq->rbq', stacked, weights, preferred_element_type=jnp.fl...  9.84 us
    while x444, local copies, waits for them, and re-layouts  6.95 us
    convert_element_type x2, other arithmetic, body(): rounded = density.astype(jnp.bfloat16)  6.44 us
    convert_element_type x24, local copies, waits for them, and re-layouts, band_matrices(): return summed.astype(jnp.bfloat16)  6.3 us
  transfers between devices with their start and end apart: 32, of which 26 were waited for; matrix products, arithmetic and copies ran while one was open for 1% of the time, Pallas kernels for 0%

profile of v1, /device:TPU:0, one launch (start us, length us, event | category | flops | bytes accessed | tf_op | source)
XLA Modules:
  0.0 132.9 jit_solution(14102285746593834437)
XLA Ops:
  2.1 3.7 %fusion.98 = bf16[6,32,512]{2,1,0:T(8,128)(2,1)S(1)} fusion(f32[]{:T(128)} %bitcast.3, s32[6,32,512]{2,1,0:T(8,128)} %param.13, f32[]{:T(128)} %bitcast.2, f32[]{:T(128)} %bitcast.1, f32[]{:T(128)} %bitcast, bf16[6,32,512]{2,1,0:T(8,128)(2,1)} %param.14), kind=kLoop, calls=%fused_computation.448 | loop fusion | flops 1376256 | bytes 786448 | tf_op jit(solution)/shard_map/convert_element_type | solution.py:121
  5.8 3.1 %collective-permute-start = (bf16[6,7,512]{2,1,0:T(8,128)(2,1)S(1)}, bf16[6,7,512]{2,1,0:T(8,128)(2,1)S(1)}, u32[]{:S(2)}, u32[]{:S(2)}) collective-permute-start(bf16[6,7,512]{2,1,0:T(8,128)(2,1)S(1)} %get-tuple-element.678), channel_id=1, source_target_pairs={{0,4},{4,8},{8,12},{12,0},{1,5},{5,9},{9,13},{13,1},{2,6},{6,10},{... | collective-permute-start | bytes 129032 | tf_op jit(solution)/shard_map/ppermute | solution.py:17
  8.9 2.1 %collective-permute-start.1 = (bf16[6,7,512]{2,1,0:T(8,128)(2,1)S(1)}, bf16[6,7,512]{2,1,0:T(8,128)(2,1)S(1)}, u32[]{:S(2)}, u32[]{:S(2)}) collective-permute-start(bf16[6,7,512]{2,1,0:T(8,128)(2,1)S(1)} %get-tuple-element.679), channel_id=1, source_target_pairs={{4,0},{8,4},{12,8},{0,12},{5,1},{9,5},{13,9},{1,13},{6,2},{10,6},{... | collective-permute-start | bytes 129032 | tf_op jit(solution)/shard_map/ppermute | solution.py:18
  11.0 2.1 %collective-permute-done = bf16[6,7,512]{2,1,0:T(8,128)(2,1)S(1)} collective-permute-done((bf16[6,7,512]{2,1,0:T(8,128)(2,1)S(1)}, bf16[6,7,512]{2,1,0:T(8,128)(2,1)S(1)}, u32[]{:S(2)}, u32[]{:S(2)}) %collective-permute-start) | collective-permute-done | bytes 43040 | tf_op jit(solution)/shard_map/ppermute | solution.py:17
  15.5 13.9 %while.62 = (s32[]{:T(128)}, f32[32,512]{1,0:T(8,128)S(1)}, bf16[6,46,640]{2,1,0:T(8,128)(2,1)S(1)}, bf16[6,15,15]{2,1,0:T(8,128)(2,1)S(1)}, s32[]{:T(128)}, /*i...) while((s32[]{:T(128)}, f32[32,512]{1,0:T(8,128)S(1)}, ...), condition=%wide.region_1.2_spmd.clone, body=%wide.region_0.1_spmd.clone.sunk | while | flops 143065104 | bytes 10342823 | solution.py:64
  29.5 5.1 %all-gather = f32[64,512]{1,0:T(8,128)S(1)} all-gather(f32[32,512]{1,0:T(8,128)S(1)} %get-tuple-element.446), channel_id=2, replica_groups=mesh['runs'=2,'gx'=4,'gy'=2,'gz'=2] {'gz'}, dimensions={0}, use_global_device_ids=true | all-gather | bytes 196608 | tf_op jit(solution)/shard_map/all_gather | solution.py:123
  34.6 3.4 %collective-permute-start.4 = (f32[1,512]{1,0:T(1,128)S(1)}, f32[1,512]{1,0:T(1,128)S(1)}, u32[]{:S(2)}, u32[]{:S(2)}) collective-permute-start(f32[1,512]{1,0:T(1,128)S(1)} %get-tuple-element.693), channel_id=1, source_target_pairs={{4,0},{8,4},{12,8},{0,12},{5,1},{9,5},{13,9},{1,13},{6,2},{10,6},{... | collective-permute-start | bytes 6152 | tf_op jit(solution)/shard_map/ppermute | solution.py:18
  39.4 4.1 %collective-permute-done.5 = f32[1,512]{1,0:T(1,128)S(1)} collective-permute-done((f32[1,512]{1,0:T(1,128)S(1)}, f32[1,512]{1,0:T(1,128)S(1)}, u32[]{:S(2)}, u32[]{:S(2)}) %collective-permute-start.5) | collective-permute-done | bytes 2080 | tf_op jit(solution)/shard_map/ppermute | solution.py:17
  45.2 3.8 %collective-permute-start.9 = (f32[3,1,512]{2,1,0:T(1,128)S(1)}, f32[3,1,512]{2,1,0:T(1,128)S(1)}, u32[]{:S(2)}, u32[]{:S(2)}) collective-permute-start(f32[3,1,512]{2,1,0:T(1,128)S(1)} %get-tuple-element.677), channel_id=1, source_target_pairs={{4,0},{8,4},{12,8},{0,12},{5,1},{9,5},{13,9},{1,13},{6,2},{10,6},{... | collective-permute-start | bytes 18440 | tf_op jit(solution)/shard_map/ppermute | solution.py:18
  49.1 1.6 %collective-permute-done.8 = f32[3,1,512]{2,1,0:T(1,128)S(1)} collective-permute-done((f32[3,1,512]{2,1,0:T(1,128)S(1)}, f32[3,1,512]{2,1,0:T(1,128)S(1)}, u32[]{:S(2)}, u32[]{:S(2)}) %collective-permute-start.8) | collective-permute-done | bytes 6176 | tf_op jit(solution)/shard_map/ppermute | solution.py:17
  52.7 3.9 %collective-permute-start.13 = (bf16[7,512]{1,0:T(8,128)(2,1)S(1)}, bf16[7,512]{1,0:T(8,128)(2,1)S(1)}, u32[]{:S(2)}, u32[]{:S(2)}) collective-permute-start(bf16[7,512]{1,0:T(8,128)(2,1)S(1)} %get-tuple-element.761), channel_id=1, source_target_pairs={{4,0},{8,4},{12,8},{0,12},{5,1},{9,5},{13,9},{1,13},{6,2},{10,6},{... | collective-permute-start | bytes 21512 | tf_op jit(solution)/shard_map/ppermute | solution.py:18
  56.6 1.6 %collective-permute-done.12 = bf16[7,512]{1,0:T(8,128)(2,1)S(1)} collective-permute-done((bf16[7,512]{1,0:T(8,128)(2,1)S(1)}, bf16[7,512]{1,0:T(8,128)(2,1)S(1)}, u32[]{:S(2)}, u32[]{:S(2)}) %collective-permute-start.12) | collective-permute-done | bytes 7200 | tf_op jit(solution)/shard_map/ppermute | solution.py:17
  60.7 7.6 %while.60 = (s32[]{:T(128)}, f32[6,32,512]{2,1,0:T(8,128)S(1)}, bf16[6,15,15]{2,1,0:T(8,128)(2,1)S(1)}, bf16[32,4,3840]{2,0,1:T(8,128)(2,1)S(1)}, s32[]{:T(128)}) while((s32[]{:T(128)}, f32[6,32,512]{2,1,0:T(8,128)S(1)}, bf16[6,15,15]{2,1,0:T(8,128)(2,1)S(1)}, bf16[32,4,3840]{2,0,1:T(8,128)(2,1)S(1)}, s32[]{:T(128)}) %tuple.339), condition=%wide.region_4.5_spmd.clone, body=%wide.region_3.4_spmd.clone.sunk | while | flops 143032320 | bytes 5378117 | solution.py:101
  68.3 2.7 %subtract_convert_fusion = bf16[6,32,512]{2,1,0:T(8,128)(2,1)S(1)} fusion(f32[6,32,512]{2,1,0:T(8,128)S(1)} %get-tuple-element.447, f32[]{:T(128)} %bitcast.3, s32[6,32,512]{2,1,0:T(8,128)S(1)} %copy-done, f32[]{:T(128)} %bitcast.2, f32[]{:T(128)} %bitcast.1, f32[]{:T(128)} %bitcast, bf16[6,32,512]{2,1,0:T(8,128)(2,1)S(1)} %copy-done.1), kind=kLoop, calls=%fused_computation.213 | loop fusion | flops 1572864 | bytes 1179664 | tf_op jit(solution)/shard_map/convert_element_type | solution.py:121
  72.2 2.8 %collective-permute-start.17 = (bf16[6,7,512]{2,1,0:T(8,128)(2,1)S(1)}, bf16[6,7,512]{2,1,0:T(8,128)(2,1)S(1)}, u32[]{:S(2)}, u32[]{:S(2)}) collective-permute-start(bf16[6,7,512]{2,1,0:T(8,128)(2,1)S(1)} %get-tuple-element.675), channel_id=1, source_target_pairs={{4,0},{8,4},{12,8},{0,12},{5,1},{9,5},{13,9},{1,13},{6,2},{10,6},{... | collective-permute-start | bytes 129032 | tf_op jit(solution)/shard_map/ppermute | solution.py:18
  75.0 2.3 %collective-permute-done.16 = bf16[6,7,512]{2,1,0:T(8,128)(2,1)S(1)} collective-permute-done((bf16[6,7,512]{2,1,0:T(8,128)(2,1)S(1)}, bf16[6,7,512]{2,1,0:T(8,128)(2,1)S(1)}, u32[]{:S(2)}, u32[]{:S(2)}) %collective-permute-start.16) | collective-permute-done | bytes 43040 | tf_op jit(solution)/shard_map/ppermute | solution.py:17
  79.3 13.9 %while.63 = (s32[]{:T(128)}, f32[32,512]{1,0:T(8,128)S(1)}, bf16[6,46,640]{2,1,0:T(8,128)(2,1)S(1)}, bf16[6,15,15]{2,1,0:T(8,128)(2,1)S(1)}, s32[]{:T(128)}, /*i...) while((s32[]{:T(128)}, f32[32,512]{1,0:T(8,128)S(1)}, ...), condition=%wide.region_6.7_spmd.clone, body=%wide.region_5.6_spmd.clone.sunk | while | flops 143065104 | bytes 10342823 | solution.py:64
  93.2 5.0 %all-gather.1 = f32[64,512]{1,0:T(8,128)S(1)} all-gather(f32[32,512]{1,0:T(8,128)S(1)} %get-tuple-element.448), channel_id=3, replica_groups=mesh['runs'=2,'gx'=4,'gy'=2,'gz'=2] {'gz'}, dimensions={0}, use_global_device_ids=true | all-gather | bytes 196608 | tf_op jit(solution)/shard_map/all_gather | solution.py:123
  98.3 3.6 %collective-permute-start.20 = (f32[1,512]{1,0:T(1,128)S(1)}, f32[1,512]{1,0:T(1,128)S(1)}, u32[]{:S(2)}, u32[]{:S(2)}) collective-permute-start(f32[1,512]{1,0:T(1,128)S(1)} %get-tuple-element.690), channel_id=1, source_target_pairs={{4,0},{8,4},{12,8},{0,12},{5,1},{9,5},{13,9},{1,13},{6,2},{10,6},{... | collective-permute-start | bytes 6152 | tf_op jit(solution)/shard_map/ppermute | solution.py:18
  103.2 4.1 %collective-permute-done.21 = f32[1,512]{1,0:T(1,128)S(1)} collective-permute-done((f32[1,512]{1,0:T(1,128)S(1)}, f32[1,512]{1,0:T(1,128)S(1)}, u32[]{:S(2)}, u32[]{:S(2)}) %collective-permute-start.21) | collective-permute-done | bytes 2080 | tf_op jit(solution)/shard_map/ppermute | solution.py:17
  109.1 3.8 %collective-permute-start.25 = (f32[3,1,512]{2,1,0:T(1,128)S(1)}, f32[3,1,512]{2,1,0:T(1,128)S(1)}, u32[]{:S(2)}, u32[]{:S(2)}) collective-permute-start(f32[3,1,512]{2,1,0:T(1,128)S(1)} %get-tuple-element.673), channel_id=1, source_target_pairs={{4,0},{8,4},{12,8},{0,12},{5,1},{9,5},{13,9},{1,13},{6,2},{10,6},{... | collective-permute-start | bytes 18440 | tf_op jit(solution)/shard_map/ppermute | solution.py:18
  112.9 1.6 %collective-permute-done.24 = f32[3,1,512]{2,1,0:T(1,128)S(1)} collective-permute-done((f32[3,1,512]{2,1,0:T(1,128)S(1)}, f32[3,1,512]{2,1,0:T(1,128)S(1)}, u32[]{:S(2)}, u32[]{:S(2)}) %collective-permute-start.24) | collective-permute-done | bytes 6176 | tf_op jit(solution)/shard_map/ppermute | solution.py:17
  116.6 3.9 %collective-permute-start.29 = (bf16[7,512]{1,0:T(8,128)(2,1)S(1)}, bf16[7,512]{1,0:T(8,128)(2,1)S(1)}, u32[]{:S(2)}, u32[]{:S(2)}) collective-permute-start(bf16[7,512]{1,0:T(8,128)(2,1)S(1)} %get-tuple-element.759), channel_id=1, source_target_pairs={{4,0},{8,4},{12,8},{0,12},{5,1},{9,5},{13,9},{1,13},{6,2},{10,6},{... | collective-permute-start | bytes 21512 | tf_op jit(solution)/shard_map/ppermute | solution.py:18
  124.6 7.6 %while.61 = (s32[]{:T(128)}, f32[6,32,512]{2,1,0:T(8,128)S(1)}, bf16[6,15,15]{2,1,0:T(8,128)(2,1)S(1)}, bf16[32,4,3840]{2,0,1:T(8,128)(2,1)S(1)}, s32[]{:T(128)}) while((s32[]{:T(128)}, f32[6,32,512]{2,1,0:T(8,128)S(1)}, bf16[6,15,15]{2,1,0:T(8,128)(2,1)S(1)}, bf16[32,4,3840]{2,0,1:T(8,128)(2,1)S(1)}, s32[]{:T(128)}) %tuple.350), condition=%wide.region_9.10_spmd.clone, body=%wide.region_8.9_spmd.clone.sunk | while | flops 143032320 | bytes 5378117 | solution.py:101
  (753 shorter events, 62.5 us)
Async XLA Ops:
  5.8 7.3 %collective-permute-start = (bf16[6,7,512]{2,1,0:T(8,128)(2,1)S(1)}, bf16[6,7,512]{2,1,0:T(8,128)(2,1)S(1)}, u32[]{:S(2)}, u32[]{:S(2)}) collective-permute-start(bf16[6,7,512]{2,1,0:T(8,128)(2,1)S(1)} %get-tuple-element.678), channel_id=1, source_target_pairs={{0,4},{4,8},{8,12},{12,0},{1,5},{5,9},{9,13},{13,1},{2,6},{6,10},{... | collective-permute-start | bytes 129032 | tf_op jit(solution)/shard_map/ppermute | solution.py:17
  8.9 4.6 %collective-permute-start.1 = (bf16[6,7,512]{2,1,0:T(8,128)(2,1)S(1)}, bf16[6,7,512]{2,1,0:T(8,128)(2,1)S(1)}, u32[]{:S(2)}, u32[]{:S(2)}) collective-permute-start(bf16[6,7,512]{2,1,0:T(8,128)(2,1)S(1)} %get-tuple-element.679), channel_id=1, source_target_pairs={{4,0},{8,4},{12,8},{0,12},{5,1},{9,5},{13,9},{1,13},{6,2},{10,6},{... | collective-permute-start | bytes 129032 | tf_op jit(solution)/shard_map/ppermute | solution.py:18
  13.7 1.3 %collective-permute-start.2 = (bf16[6,46,7]{2,1,0:T(8,128)(2,1)S(1)}, bf16[6,46,7]{2,1,0:T(8,128)(2,1)S(1)}, u32[]{:S(2)}, u32[]{:S(2)}) collective-permute-start(bf16[6,46,7]{2,1,0:T(8,128)(2,1)S(1)} %get-tuple-element.662), channel_id=1, source_target_pairs={{0,2},{2,0},{1,3},{3,1},{4,6},{6,4},{5,7},{7,5},{8,10},{10,8},{9,1... | collective-permute-start | bytes 11600 | tf_op jit(solution)/shard_map/ppermute | solution.py:17
  13.8 1.4 %collective-permute-start.3 = (bf16[6,46,7]{2,1,0:T(8,128)(2,1)S(1)}, bf16[6,46,7]{2,1,0:T(8,128)(2,1)S(1)}, u32[]{:S(2)}, u32[]{:S(2)}) collective-permute-start(bf16[6,46,7]{2,1,0:T(8,128)(2,1)S(1)} %get-tuple-element.663), channel_id=1, source_target_pairs={{2,0},{0,2},{3,1},{1,3},{6,4},{4,6},{7,5},{5,7},{10,8},{8,10},{11,... | collective-permute-start | bytes 11600 | tf_op jit(solution)/shard_map/ppermute | solution.py:18
  34.6 4.7 %collective-permute-start.4 = (f32[1,512]{1,0:T(1,128)S(1)}, f32[1,512]{1,0:T(1,128)S(1)}, u32[]{:S(2)}, u32[]{:S(2)}) collective-permute-start(f32[1,512]{1,0:T(1,128)S(1)} %get-tuple-element.693), channel_id=1, source_target_pairs={{4,0},{8,4},{12,8},{0,12},{5,1},{9,5},{13,9},{1,13},{6,2},{10,6},{... | collective-permute-start | bytes 6152 | tf_op jit(solution)/shard_map/ppermute | solution.py:18
  38.0 5.4 %collective-permute-start.5 = (f32[1,512]{1,0:T(1,128)S(1)}, f32[1,512]{1,0:T(1,128)S(1)}, u32[]{:S(2)}, u32[]{:S(2)}) collective-permute-start(f32[1,512]{1,0:T(1,128)S(1)} %get-tuple-element.692), channel_id=1, source_target_pairs={{0,4},{4,8},{8,12},{12,0},{1,5},{5,9},{9,13},{13,1},{2,6},{6,10},{... | collective-permute-start | bytes 6152 | tf_op jit(solution)/shard_map/ppermute | solution.py:17
  43.5 1.3 %collective-permute-start.7 = (f32[34,1]{1,0:T(8,128)S(1)}, f32[34,1]{1,0:T(8,128)S(1)}, u32[]{:S(2)}, u32[]{:S(2)}) collective-permute-start(f32[34,1]{1,0:T(8,128)S(1)} %get-tuple-element.687), channel_id=1, source_target_pairs={{0,2},{2,0},{1,3},{3,1},{4,6},{6,4},{5,7},{7,5},{8,10},{10,8},{9,1... | collective-permute-start | bytes 416 | tf_op jit(solution)/shard_map/ppermute | solution.py:17
  45.2 5.5 %collective-permute-start.8 = (f32[3,1,512]{2,1,0:T(1,128)S(1)}, f32[3,1,512]{2,1,0:T(1,128)S(1)}, u32[]{:S(2)}, u32[]{:S(2)}) collective-permute-start(f32[3,1,512]{2,1,0:T(1,128)S(1)} %get-tuple-element.676), channel_id=1, source_target_pairs={{0,4},{4,8},{8,12},{12,0},{1,5},{5,9},{9,13},{13,1},{2,6},{6,10},{... | collective-permute-start | bytes 18440 | tf_op jit(solution)/shard_map/ppermute | solution.py:17
  45.2 5.4 %collective-permute-start.9 = (f32[3,1,512]{2,1,0:T(1,128)S(1)}, f32[3,1,512]{2,1,0:T(1,128)S(1)}, u32[]{:S(2)}, u32[]{:S(2)}) collective-permute-start(f32[3,1,512]{2,1,0:T(1,128)S(1)} %get-tuple-element.677), channel_id=1, source_target_pairs={{4,0},{8,4},{12,8},{0,12},{5,1},{9,5},{13,9},{1,13},{6,2},{10,6},{... | collective-permute-start | bytes 18440 | tf_op jit(solution)/shard_map/ppermute | solution.py:18
  50.8 1.4 %collective-permute-start.11 = (f32[3,34,1]{2,1,0:T(8,128)S(1)}, f32[3,34,1]{2,1,0:T(8,128)S(1)}, u32[]{:S(2)}, u32[]{:S(2)}) collective-permute-start(f32[3,34,1]{2,1,0:T(8,128)S(1)} %get-tuple-element.667), channel_id=1, source_target_pairs={{2,0},{0,2},{3,1},{1,3},{6,4},{4,6},{7,5},{5,7},{10,8},{8,10},{11,... | collective-permute-start | bytes 1232 | tf_op jit(solution)/shard_map/ppermute | solution.py:18
  52.7 5.5 %collective-permute-start.12 = (bf16[7,512]{1,0:T(8,128)(2,1)S(1)}, bf16[7,512]{1,0:T(8,128)(2,1)S(1)}, u32[]{:S(2)}, u32[]{:S(2)}) collective-permute-start(bf16[7,512]{1,0:T(8,128)(2,1)S(1)} %get-tuple-element.760), channel_id=1, source_target_pairs={{0,4},{4,8},{8,12},{12,0},{1,5},{5,9},{9,13},{13,1},{2,6},{6,10},{... | collective-permute-start | bytes 21512 | tf_op jit(solution)/shard_map/ppermute | solution.py:17
  52.7 5.5 %collective-permute-start.13 = (bf16[7,512]{1,0:T(8,128)(2,1)S(1)}, bf16[7,512]{1,0:T(8,128)(2,1)S(1)}, u32[]{:S(2)}, u32[]{:S(2)}) collective-permute-start(bf16[7,512]{1,0:T(8,128)(2,1)S(1)} %get-tuple-element.761), channel_id=1, source_target_pairs={{4,0},{8,4},{12,8},{0,12},{5,1},{9,5},{13,9},{1,13},{6,2},{10,6},{... | collective-permute-start | bytes 21512 | tf_op jit(solution)/shard_map/ppermute | solution.py:18
  71.1 6.3 %collective-permute-start.16 = (bf16[6,7,512]{2,1,0:T(8,128)(2,1)S(1)}, bf16[6,7,512]{2,1,0:T(8,128)(2,1)S(1)}, u32[]{:S(2)}, u32[]{:S(2)}) collective-permute-start(bf16[6,7,512]{2,1,0:T(8,128)(2,1)S(1)} %get-tuple-element.674), channel_id=1, source_target_pairs={{0,4},{4,8},{8,12},{12,0},{1,5},{5,9},{9,13},{13,1},{2,6},{6,10},{... | collective-permute-start | bytes 129032 | tf_op jit(solution)/shard_map/ppermute | solution.py:17
  72.2 5.1 %collective-permute-start.17 = (bf16[6,7,512]{2,1,0:T(8,128)(2,1)S(1)}, bf16[6,7,512]{2,1,0:T(8,128)(2,1)S(1)}, u32[]{:S(2)}, u32[]{:S(2)}) collective-permute-start(bf16[6,7,512]{2,1,0:T(8,128)(2,1)S(1)} %get-tuple-element.675), channel_id=1, source_target_pairs={{4,0},{8,4},{12,8},{0,12},{5,1},{9,5},{13,9},{1,13},{6,2},{10,6},{... | collective-permute-start | bytes 129032 | tf_op jit(solution)/shard_map/ppermute | solution.py:18
  77.5 1.3 %collective-permute-start.18 = (bf16[6,46,7]{2,1,0:T(8,128)(2,1)S(1)}, bf16[6,46,7]{2,1,0:T(8,128)(2,1)S(1)}, u32[]{:S(2)}, u32[]{:S(2)}) collective-permute-start(bf16[6,46,7]{2,1,0:T(8,128)(2,1)S(1)} %get-tuple-element.660), channel_id=1, source_target_pairs={{0,2},{2,0},{1,3},{3,1},{4,6},{6,4},{5,7},{7,5},{8,10},{10,8},{9,1... | collective-permute-start | bytes 11600 | tf_op jit(solution)/shard_map/ppermute | solution.py:17
  77.6 1.4 %collective-permute-start.19 = (bf16[6,46,7]{2,1,0:T(8,128)(2,1)S(1)}, bf16[6,46,7]{2,1,0:T(8,128)(2,1)S(1)}, u32[]{:S(2)}, u32[]{:S(2)}) collective-permute-start(bf16[6,46,7]{2,1,0:T(8,128)(2,1)S(1)} %get-tuple-element.661), channel_id=1, source_target_pairs={{2,0},{0,2},{3,1},{1,3},{6,4},{4,6},{7,5},{5,7},{10,8},{8,10},{11,... | collective-permute-start | bytes 11600 | tf_op jit(solution)/shard_map/ppermute | solution.py:18
  98.3 4.9 %collective-permute-start.20 = (f32[1,512]{1,0:T(1,128)S(1)}, f32[1,512]{1,0:T(1,128)S(1)}, u32[]{:S(2)}, u32[]{:S(2)}) collective-permute-start(f32[1,512]{1,0:T(1,128)S(1)} %get-tuple-element.690), channel_id=1, source_target_pairs={{4,0},{8,4},{12,8},{0,12},{5,1},{9,5},{13,9},{1,13},{6,2},{10,6},{... | collective-permute-start | bytes 6152 | tf_op jit(solution)/shard_map/ppermute | solution.py:18
  101.9 5.4 %collective-permute-start.21 = (f32[1,512]{1,0:T(1,128)S(1)}, f32[1,512]{1,0:T(1,128)S(1)}, u32[]{:S(2)}, u32[]{:S(2)}) collective-permute-start(f32[1,512]{1,0:T(1,128)S(1)} %get-tuple-element.689), channel_id=1, source_target_pairs={{0,4},{4,8},{8,12},{12,0},{1,5},{5,9},{9,13},{13,1},{2,6},{6,10},{... | collective-permute-start | bytes 6152 | tf_op jit(solution)/shard_map/ppermute | solution.py:17
  107.4 1.3 %collective-permute-start.23 = (f32[34,1]{1,0:T(8,128)S(1)}, f32[34,1]{1,0:T(8,128)S(1)}, u32[]{:S(2)}, u32[]{:S(2)}) collective-permute-start(f32[34,1]{1,0:T(8,128)S(1)} %get-tuple-element.683), channel_id=1, source_target_pairs={{0,2},{2,0},{1,3},{3,1},{4,6},{6,4},{5,7},{7,5},{8,10},{10,8},{9,1... | collective-permute-start | bytes 416 | tf_op jit(solution)/shard_map/ppermute | solution.py:17
  109.0 5.5 %collective-permute-start.24 = (f32[3,1,512]{2,1,0:T(1,128)S(1)}, f32[3,1,512]{2,1,0:T(1,128)S(1)}, u32[]{:S(2)}, u32[]{:S(2)}) collective-permute-start(f32[3,1,512]{2,1,0:T(1,128)S(1)} %get-tuple-element.672), channel_id=1, source_target_pairs={{0,4},{4,8},{8,12},{12,0},{1,5},{5,9},{9,13},{13,1},{2,6},{6,10},{... | collective-permute-start | bytes 18440 | tf_op jit(solution)/shard_map/ppermute | solution.py:17
  109.1 5.4 %collective-permute-start.25 = (f32[3,1,512]{2,1,0:T(1,128)S(1)}, f32[3,1,512]{2,1,0:T(1,128)S(1)}, u32[]{:S(2)}, u32[]{:S(2)}) collective-permute-start(f32[3,1,512]{2,1,0:T(1,128)S(1)} %get-tuple-element.673), channel_id=1, source_target_pairs={{4,0},{8,4},{12,8},{0,12},{5,1},{9,5},{13,9},{1,13},{6,2},{10,6},{... | collective-permute-start | bytes 18440 | tf_op jit(solution)/shard_map/ppermute | solution.py:18
  114.7 1.4 %collective-permute-start.27 = (f32[3,34,1]{2,1,0:T(8,128)S(1)}, f32[3,34,1]{2,1,0:T(8,128)S(1)}, u32[]{:S(2)}, u32[]{:S(2)}) collective-permute-start(f32[3,34,1]{2,1,0:T(8,128)S(1)} %get-tuple-element.665), channel_id=1, source_target_pairs={{2,0},{0,2},{3,1},{1,3},{6,4},{4,6},{7,5},{5,7},{10,8},{8,10},{11,... | collective-permute-start | bytes 1232 | tf_op jit(solution)/shard_map/ppermute | solution.py:18
  116.5 5.5 %collective-permute-start.28 = (bf16[7,512]{1,0:T(8,128)(2,1)S(1)}, bf16[7,512]{1,0:T(8,128)(2,1)S(1)}, u32[]{:S(2)}, u32[]{:S(2)}) collective-permute-start(bf16[7,512]{1,0:T(8,128)(2,1)S(1)} %get-tuple-element.758), channel_id=1, source_target_pairs={{0,4},{4,8},{8,12},{12,0},{1,5},{5,9},{9,13},{13,1},{2,6},{6,10},{... | collective-permute-start | bytes 21512 | tf_op jit(solution)/shard_map/ppermute | solution.py:17
  116.6 5.5 %collective-permute-start.29 = (bf16[7,512]{1,0:T(8,128)(2,1)S(1)}, bf16[7,512]{1,0:T(8,128)(2,1)S(1)}, u32[]{:S(2)}, u32[]{:S(2)}) collective-permute-start(bf16[7,512]{1,0:T(8,128)(2,1)S(1)} %get-tuple-element.759), channel_id=1, source_target_pairs={{4,0},{8,4},{12,8},{0,12},{5,1},{9,5},{13,9},{1,13},{6,2},{10,6},{... | collective-permute-start | bytes 21512 | tf_op jit(solution)/shard_map/ppermute | solution.py:18
  (13 other events, 55.0 us)
